TPU v7x, 32 devices: a whole 2x2x4 slice. The times are simulated.
32 devices in a mesh: dp: 16 (over z, x, core), tensor: 2 (over y).
Axes of the slice: x: 2, y: 2, z: 4, core: 2. Of those that a mesh axis runs over, the one named last changes fastest.
Arguments:
- tokens: bfloat16 [16384, 1024], P(('dp', 'tensor')), may hold values from -6 to 6
- cotangent: bfloat16 [16384, 1024], P(('dp', 'tensor')), may hold values from -6 to 6
- gain_one: float32 [1024], replicated, may hold values from 0.1 to 1.9
- bias_one: float32 [1024], replicated, may hold values from -3 to 3
- w_qkv: bfloat16 [1024, 3, 1024], P(None, None, 'tensor'), may hold values from -0.1875 to 0.1875
- bias_qv: float32 [2, 1024], P(None, 'tensor'), may hold values from -3 to 3
- w_out: bfloat16 [1024, 1024], P('tensor'), may hold values from -3 to 3
- out_bias: float32 [1024], replicated, may hold values from -4 to 4
- gain_two: float32 [1024], replicated, may hold values from 0.1 to 1.9
- bias_two: float32 [1024], replicated, may hold values from -3 to 3
- w_fc: bfloat16 [1024, 4096], P(None, 'tensor'), may hold values from -0.1875 to 0.1875
- fc_bias: float32 [4096], P('tensor'), may hold values from -3 to 3
- w_proj: bfloat16 [4096, 1024], P('tensor'), may hold values from -0.5 to 0.5
- proj_bias: float32 [1024], replicated, may hold values from -4 to 4
Outputs:
- block_out: bfloat16 [2, 16384, 1024], P(None, ('dp', 'tensor'))
- grad_tokens: float32 [2, 16384, 1024], P(None, ('dp', 'tensor'))
- grad_gain_one: float32 [2, 1024], replicated
- grad_bias_one: float32 [2, 1024], replicated
- grad_w_qkv: float32 [2, 1024, 3, 1024], P(None, None, None, 'tensor')
- grad_bias_qv: float32 [2, 2, 1024], P(None, None, 'tensor')
- grad_w_out: float32 [2, 1024, 1024], P(None, 'tensor')
- grad_out_bias: float32 [2, 1024], replicated
- grad_gain_two: float32 [2, 1024], replicated
- grad_bias_two: float32 [2, 1024], replicated
- grad_w_fc: float32 [2, 1024, 4096], P(None, None, 'tensor')
- grad_fc_bias: float32 [2, 4096], P(None, 'tensor')
- grad_w_proj: float32 [2, 4096, 1024], P(None, 'tensor')
- grad_proj_bias: float32 [2, 1024], replicated
All inputs are finite; a program needn't handle non-finite values.
Results may differ from a plain program's by a relative error of at most 0.012.
The roundings to bfloat16 on the way count: a program that leaves them out, or rounds other values in their place, can miss the bound.
Values may be sent and summed in bfloat16 or wider, within the bound.
No kernel may reach another device: no remote copies, remote signals or barrier semaphores. Data moves between devices by JAX's collectives and lax.ppermute only.
A program may use at most 320 MiB of HBM per device.

v0:
```python
from functools import partial

import jax
import jax.numpy as jnp
from jax import lax
from jax.sharding import PartitionSpec as P

HEAD = 64
LEN = 1024
DEPTH_A = 12
DEPTH_B = 48


def norm_layer(values, norm_gain, norm_bias):
    centre = values - jnp.mean(values, axis=-1, keepdims=True)
    spread = jnp.mean(centre * centre, axis=-1, keepdims=True)
    return centre * lax.rsqrt(spread + 1e-05) * norm_gain + norm_bias


def causal_mask(first, block_rows, limit):
    query_pos = first + jnp.arange(block_rows, dtype=jnp.int32)
    key_pos = jnp.arange(limit, dtype=jnp.int32)
    return (key_pos[None, :] <= query_pos[:, None])[None, None]


def attend_forward(queries, key_rows, value_rows):
    length = queries.shape[1]
    block_rows = min(512, length)
    mixed_parts = []
    lse_parts = []
    for block_index in range(length // block_rows):
        first = block_index * block_rows
        limit = first + block_rows
        query_rows = queries[:, first:limit]
        scores = 0.125 * jnp.einsum(
            "sqhe,skhe->shqk", query_rows, key_rows[:, :limit], preferred_element_type=jnp.float32
        )
        scores = jnp.where(causal_mask(first, block_rows, limit), scores, -1e30)
        highest = jnp.max(scores, axis=-1, keepdims=True)
        raised = jnp.exp(scores - highest)
        totals = jnp.sum(raised, axis=-1, keepdims=True)
        probabilities = (raised / totals).astype(jnp.bfloat16)
        mixed_parts.append(
            jnp.einsum(
                "shqk,skhe->sqhe",
                probabilities,
                value_rows[:, :limit],
                preferred_element_type=jnp.float32,
            ).astype(jnp.bfloat16)
        )
        lse_parts.append((highest + jnp.log(totals))[..., 0])
    return (jnp.concatenate(mixed_parts, axis=1), jnp.concatenate(lse_parts, axis=2))


def attend_backward(queries, key_rows, value_rows, log_totals, grad_mixed):
    length = queries.shape[1]
    block_rows = min(512, length)
    grad_keys = jnp.zeros(key_rows.shape, jnp.float32)
    grad_values = jnp.zeros(value_rows.shape, jnp.float32)
    grad_query_parts = []
    for block_index in range(length // block_rows):
        first = block_index * block_rows
        limit = first + block_rows
        query_rows = queries[:, first:limit]
        allowed = causal_mask(first, block_rows, limit)
        scores = 0.125 * jnp.einsum(
            "sqhe,skhe->shqk", query_rows, key_rows[:, :limit], preferred_element_type=jnp.float32
        )
        scores = jnp.where(allowed, scores, -1e30)
        probabilities = jnp.exp(scores - log_totals[:, :, first:limit, None])
        grad_rows = grad_mixed[:, first:limit]
        grad_probs = jnp.einsum(
            "sqhe,skhe->shqk", grad_rows, value_rows[:, :limit], preferred_element_type=jnp.float32
        )
        centre = jnp.sum(probabilities * grad_probs, axis=-1, keepdims=True)
        grad_scores = jnp.where(allowed, probabilities * (grad_probs - centre), 0.0).astype(
            jnp.bfloat16
        )
        grad_query_parts.append(
            0.125
            * jnp.einsum(
                "shqk,skhe->sqhe",
                grad_scores,
                key_rows[:, :limit],
                preferred_element_type=jnp.float32,
            )
        )
        grad_keys = grad_keys.at[:, :limit].add(
            0.125
            * jnp.einsum(
                "shqk,sqhe->skhe", grad_scores, query_rows, preferred_element_type=jnp.float32
            )
        )
        grad_values = grad_values.at[:, :limit].add(
            jnp.einsum(
                "shqk,sqhe->skhe",
                probabilities.astype(jnp.bfloat16),
                grad_rows,
                preferred_element_type=jnp.float32,
            )
        )
    return (jnp.concatenate(grad_query_parts, axis=1), grad_keys, grad_values)


def row_total(values):
    return jnp.sum(values.astype(jnp.float32), axis=0)


def per_device(
    tokens,
    cotangent,
    gain_one,
    bias_one,
    w_qkv,
    bias_qv,
    w_out,
    out_bias,
    gain_two,
    bias_two,
    w_fc,
    fc_bias,
    w_proj,
    proj_bias,
):
    residual = tokens.astype(jnp.float32)
    upstream = cotangent.astype(jnp.float32)
    head_cols = w_qkv.shape[2]
    local_heads = head_cols // HEAD
    collected = []
    for depth_count in (DEPTH_A, DEPTH_B):
        branch_scale = float(depth_count) ** (-0.5)
        normed, norm_back_one = jax.vjp(norm_layer, residual, gain_one, bias_one)
        normed_all = lax.all_gather(normed.astype(jnp.bfloat16), "tensor", axis=0, tiled=True)
        all_rows = normed_all.shape[0]
        seq_count = all_rows // LEN

        def heads_of(flat):
            return flat.reshape(seq_count, LEN, local_heads, HEAD)

        projected = jnp.einsum("td,dcf->tcf", normed_all, w_qkv, preferred_element_type=jnp.float32)
        queries = heads_of((projected[:, 0] + bias_qv[0]).astype(jnp.bfloat16))
        key_rows = heads_of(projected[:, 1].astype(jnp.bfloat16))
        value_rows = heads_of((projected[:, 2] + bias_qv[1]).astype(jnp.bfloat16))
        mixed, log_totals = attend_forward(queries, key_rows, value_rows)
        mixed_flat = mixed.reshape(all_rows, head_cols)
        branch_terms = jnp.dot(mixed_flat, w_out, preferred_element_type=jnp.float32)
        branch = (
            lax.psum_scatter(branch_terms, "tensor", scatter_dimension=0, tiled=True) + out_bias
        )
        middle = residual + branch_scale * branch
        normed_two, norm_back_two = jax.vjp(norm_layer, middle, gain_two, bias_two)
        normed_two_all = lax.all_gather(
            normed_two.astype(jnp.bfloat16), "tensor", axis=0, tiled=True
        )
        hidden = jnp.dot(normed_two_all, w_fc, preferred_element_type=jnp.float32) + fc_bias
        active, gelu_back = jax.vjp(partial(jax.nn.gelu, approximate=True), hidden)
        active_low = active.astype(jnp.bfloat16)
        second_terms = jnp.dot(active_low, w_proj, preferred_element_type=jnp.float32)
        second = (
            lax.psum_scatter(second_terms, "tensor", scatter_dimension=0, tiled=True) + proj_bias
        )
        output = middle + branch_scale * second
        grad_second = (branch_scale * upstream).astype(jnp.bfloat16)
        grad_proj_bias = row_total(grad_second)
        grad_second_all = lax.all_gather(grad_second, "tensor", axis=0, tiled=True)
        grad_w_proj = jnp.einsum(
            "tf,td->fd", active_low, grad_second_all, preferred_element_type=jnp.float32
        )
        grad_active = jnp.einsum(
            "td,fd->tf", grad_second_all, w_proj, preferred_element_type=jnp.float32
        )
        grad_hidden = gelu_back(grad_active)[0].astype(jnp.bfloat16)
        grad_fc_bias = row_total(grad_hidden)
        grad_w_fc = jnp.einsum(
            "td,tf->df", normed_two_all, grad_hidden, preferred_element_type=jnp.float32
        )
        grad_normed_terms = jnp.einsum(
            "tf,df->td", grad_hidden, w_fc, preferred_element_type=jnp.float32
        )
        grad_normed_two = lax.psum_scatter(
            grad_normed_terms, "tensor", scatter_dimension=0, tiled=True
        )
        grad_middle_norm, grad_gain_two, grad_bias_two = norm_back_two(grad_normed_two)
        grad_middle = upstream + grad_middle_norm
        grad_branch = (branch_scale * grad_middle).astype(jnp.bfloat16)
        grad_out_bias = row_total(grad_branch)
        grad_branch_all = lax.all_gather(grad_branch, "tensor", axis=0, tiled=True)
        grad_w_out = jnp.einsum(
            "tf,td->fd", mixed_flat, grad_branch_all, preferred_element_type=jnp.float32
        )
        grad_mixed = jnp.einsum(
            "td,fd->tf", grad_branch_all, w_out, preferred_element_type=jnp.float32
        ).astype(jnp.bfloat16)
        grad_query, grad_keys, grad_values = attend_backward(
            queries, key_rows, value_rows, log_totals, heads_of(grad_mixed)
        )
        grad_stacked = jnp.stack(
            [
                grad_query.reshape(all_rows, head_cols),
                grad_keys.reshape(all_rows, head_cols),
                grad_values.reshape(all_rows, head_cols),
            ],
            axis=1,
        ).astype(jnp.bfloat16)
        grad_bias_qv = jnp.stack([row_total(grad_stacked[:, 0]), row_total(grad_stacked[:, 2])])
        grad_w_qkv = jnp.einsum(
            "td,tcf->dcf", normed_all, grad_stacked, preferred_element_type=jnp.float32
        )
        grad_normed_terms_one = jnp.einsum(
            "tcf,dcf->td", grad_stacked, w_qkv, preferred_element_type=jnp.float32
        )
        grad_normed = lax.psum_scatter(
            grad_normed_terms_one, "tensor", scatter_dimension=0, tiled=True
        )
        grad_input_norm, grad_gain_one, grad_bias_one = norm_back_one(grad_normed)
        grad_input = grad_middle + grad_input_norm
        weight_part = (grad_w_qkv, grad_bias_qv, grad_w_out, grad_w_fc, grad_fc_bias, grad_w_proj)
        small_part = (
            grad_gain_one,
            grad_bias_one,
            grad_out_bias,
            grad_gain_two,
            grad_bias_two,
            grad_proj_bias,
        )
        weight_part = lax.psum(
            (
                weight_part[0],
                weight_part[1],
                weight_part[2],
                weight_part[3],
                weight_part[4],
                weight_part[5],
            ),
            "dp",
        )
        small_part = lax.psum(
            (
                small_part[0],
                small_part[1],
                small_part[2],
                small_part[3],
                small_part[4],
                small_part[5],
            ),
            ("dp", "tensor"),
        )
        collected.append((output.astype(jnp.bfloat16), grad_input, weight_part, small_part))
    weight_stack = tuple(
        (jnp.stack([entry[2][index] for entry in collected]) for index in range(6))
    )
    small_stack = tuple((jnp.stack([entry[3][index] for entry in collected]) for index in range(6)))
    block_out = jnp.stack([entry[0] for entry in collected])
    grad_tokens = jnp.stack([entry[1] for entry in collected])
    return (
        block_out,
        grad_tokens,
        small_stack[0],
        small_stack[1],
        weight_stack[0],
        weight_stack[1],
        weight_stack[2],
        small_stack[2],
        small_stack[3],
        small_stack[4],
        weight_stack[3],
        weight_stack[4],
        weight_stack[5],
        small_stack[5],
    )


def solution(mesh):
    return jax.shard_map(
        per_device,
        mesh=mesh,
        in_specs=(
            P(("dp", "tensor"), None),
            P(("dp", "tensor"), None),
            P(),
            P(),
            P(None, None, "tensor"),
            P(None, "tensor"),
            P("tensor", None),
            P(),
            P(),
            P(),
            P(None, "tensor"),
            P("tensor"),
            P("tensor", None),
            P(),
        ),
        out_specs=(
            P(None, ("dp", "tensor"), None),
            P(None, ("dp", "tensor"), None),
            P(),
            P(),
            P(None, None, None, "tensor"),
            P(None, None, "tensor"),
            P(None, "tensor", None),
            P(),
            P(),
            P(),
            P(None, None, "tensor"),
            P(None, "tensor"),
            P(None, "tensor", None),
            P(),
        ),
        check_vma=False,
    )
```

profile of v0, /device:TPU:0, one launch (start us, length us, event | category | flops | bytes accessed | tf_op | source)
XLA Modules:
  0.0 1710.2 jit_solution(3722719060411372720)
XLA Ops:
  16.6 33.7 %all-gather.8.cloned.1.call-done = bf16[1024,1024]{1,0:T(8,128)(2,1)} async-done(((bf16[512,1024]{1,0:T(8,128)(2,1)}), bf16[1024,1024]{1,0:T(8,128)(2,1)}) %all-gather.8.cloned.1.call-update) | async-done | bytes 2097168 | tf_op jit(solution)/shard_map/all_gather | solution.py:133
  82.7 54.5 %reduce-scatter.8.cloned.1.call-done = f32[512,1024]{1,0:T(8,128)} async-done(((f32[1024,1024]{1,0:T(8,128)}), f32[512,1024]{1,0:T(8,128)}) %reduce-scatter.8.cloned.1.call-update) | async-done | bytes 2097168 | tf_op jit(solution)/shard_map/reduce_scatter | solution.py:148
  146.2 30.3 %all-gather.10.cloned.1.call-done = bf16[1024,1024]{1,0:T(8,128)(2,1)} async-done(((bf16[512,1024]{1,0:T(8,128)(2,1)}), bf16[1024,1024]{1,0:T(8,128)(2,1)}) %all-gather.10.cloned.1.call-update) | async-done | bytes 2097168 | tf_op jit(solution)/shard_map/all_gather | solution.py:152
  176.5 10.9 fusion.207
  187.4 24.2 %all-gather.14.cloned.1.call-done = bf16[1024,1024]{1,0:T(8,128)(2,1)} async-done(((bf16[512,1024]{1,0:T(8,128)(2,1)}), bf16[1024,1024]{1,0:T(8,128)(2,1)}) %all-gather.14.cloned.1.call-update) | async-done | bytes 2097168 | tf_op jit(solution)/shard_map/all_gather | solution.py:165
  211.6 13.9 convert_reduce_fusion.1
  233.7 12.0 fusion.195
  246.5 41.5 %reduce-scatter.14.cloned.1.call-done = f32[512,1024]{1,0:T(8,128)} async-done(((f32[1024,1024]{1,0:T(8,128)}), f32[512,1024]{1,0:T(8,128)}) %reduce-scatter.14.cloned.1.call-update) | async-done | bytes 2097168 | tf_op jit(solution)/shard_map/reduce_scatter | solution.py:180
  291.6 53.6 %reduce-scatter.10.cloned.1.call-done = f32[512,1024]{1,0:T(8,128)} async-done(((f32[1024,1024]{1,0:T(8,128)}), f32[512,1024]{1,0:T(8,128)}) %reduce-scatter.10.cloned.1.call-update) | async-done | bytes 2097168 | tf_op jit(solution)/shard_map/reduce_scatter | solution.py:160
  353.8 26.6 %all-gather.12.cloned.1.call-done = bf16[1024,1024]{1,0:T(8,128)(2,1)} async-done(((bf16[512,1024]{1,0:T(8,128)(2,1)}), bf16[1024,1024]{1,0:T(8,128)(2,1)}) %all-gather.12.cloned.1.call-update) | async-done | bytes 2097168 | tf_op jit(solution)/shard_map/all_gather | solution.py:152
  380.4 10.9 fusion.208
  391.6 24.1 %all-gather.18.cloned.1.call-done = bf16[1024,1024]{1,0:T(8,128)(2,1)} async-done(((bf16[512,1024]{1,0:T(8,128)(2,1)}), bf16[1024,1024]{1,0:T(8,128)(2,1)}) %all-gather.18.cloned.1.call-update) | async-done | bytes 2097168 | tf_op jit(solution)/shard_map/all_gather | solution.py:165
  415.7 13.8 convert_reduce_fusion
  437.6 12.0 fusion.196
  459.7 14.5 fusion.160
  474.2 10.0 fusion.169
  484.2 32.8 %fusion.154 = bf16[1,512,8,64]{1,3,2,0:T(8,128)(2,1)} fusion(bf16[1024,8,64]{0,2,1:T(8,128)(2,1)} %bitcast.230, f32[8,512,1024]{2,1,0:T(8,128)} %fusion.169, pred[512,1024]{1,0:T(8,128)(4,1)} %iota_compare_fusion, f32[8,512,1024]{2,1,0:T(8,128)} %copy-done.1, f32[8,512]{1,0:T(8,128)S(1)} %log_add_fusion), kind=kOutput, calls=%fused_computation.178 | convolution fusion | flops 583537664 | bytes 35667968 | tf_op jit(solution)/shard_map/shqk,skhe->sqhe/dot_general | solution.py:81
  521.8 15.1 fusion.127
  547.5 17.9 %reduce-scatter.12.cloned.1.call-done = f32[512,1024]{1,0:T(8,128)} async-done(((f32[1024,1024]{1,0:T(8,128)}), f32[512,1024]{1,0:T(8,128)}) %reduce-scatter.12.cloned.1.call-update) | async-done | bytes 2097168 | tf_op jit(solution)/shard_map/reduce_scatter | solution.py:160
  573.6 33.6 %fusion.89 = bf16[1,1024,8,64]{1,3,2,0:T(8,128)(2,1)} fusion(f32[1,512,8,64]{1,3,2,0:T(8,128)} %fusion.127, f32[8,512,1024]{2,1,0:T(8,128)} %fusion.169, pred[512,1024]{1,0:T(8,128)(4,1)} %iota_compare_fusion, bf16[1,1024,8,64]{1,3,2,0:T(8,128)(2,1)} %copy-done.26, f32[8,512,1024]{2,1,0:T(8,128)} %copy-done.1, f32[8,512]{1,0:T(8,128)S(1)} %log_add_fusion), kind=kOutput, calls=%fused_computation.122 | convolution fusion | flops 584586240 | bytes 70811648 | tf_op jit(solution)/shard_map/shqk,sqhe->skhe/dot_general | solution.py:90
  637.3 14.4 fusion.157
  651.7 9.9 fusion.171
  661.6 32.8 %fusion.151 = bf16[1,512,8,64]{1,3,2,0:T(8,128)(2,1)} fusion(bf16[1024,8,64]{0,2,1:T(8,128)(2,1)} %bitcast.232, f32[8,512,1024]{2,1,0:T(8,128)} %fusion.171, pred[512,1024]{1,0:T(8,128)(4,1)} %iota_compare_fusion, f32[8,512,1024]{2,1,0:T(8,128)} %copy-done.1, f32[8,512]{1,0:T(8,128)S(1)} %log_add_fusion), kind=kOutput, calls=%fused_computation.177 | convolution fusion | flops 583537664 | bytes 35667968 | tf_op jit(solution)/shard_map/shqk,skhe->sqhe/dot_general | solution.py:81
  699.1 14.5 fusion.118
  713.5 34.0 %fusion.87 = bf16[1,1024,8,64]{1,3,2,0:T(8,128)(2,1)} fusion(f32[1,512,8,64]{1,3,2,0:T(8,128)} %fusion.118, f32[8,512,1024]{2,1,0:T(8,128)} %fusion.171, pred[512,1024]{1,0:T(8,128)(4,1)} %iota_compare_fusion, bf16[1,1024,8,64]{1,3,2,0:T(8,128)(2,1)} %copy-done.26, f32[8,512,1024]{2,1,0:T(8,128)} %copy-done.1, f32[8,512]{1,0:T(8,128)S(1)} %log_add_fusion), kind=kOutput, calls=%fused_computation.118 | convolution fusion | flops 584586240 | bytes 70811648 | tf_op jit(solution)/shard_map/shqk,sqhe->skhe/dot_general | solution.py:90
  774.2 10.9 convolution_bitcast_fusion.3
  785.2 13.2 convolution_bitcast_fusion.1
  838.9 65.0 %all-reduce.5 = (f32[1,2,512]{2,1,0:T(2,128)S(1)}, f32[1,2,512]{2,1,0:T(2,128)S(1)}, f32[1,2048]{1,0:T(1,128)S(1)}, f32[1,2048]{1,0:T(1,128)S(1)}) all-reduce(f32[1,2,512]{2,1,0:T(2,128)S(1)} %maximum_bitcast_fusion.1, f32[1,2,512]{2,1,0:T(2,128)S(1)} %maximum_bitcast_fusion, ...), channel_id=1, replica_groups=mesh['dp'=16,'tensor'=2] {'dp'}, use_global_device_ids=true, to_apply=%region_44.45 | all-reduce | flops 6144 | bytes 49152 | tf_op jit(solution)/shard_map/psum | solution.py:226
  917.2 39.3 %all-reduce.4 = (f32[1,1024]{1,0:T(1,128)S(1)}, f32[1,1024]{1,0:T(1,128)S(1)}, f32[1,1024]{1,0:T(1,128)S(1)}, f32[1,1024]{1,0:T(1,128)S(1)}, f32[1,1024]{1,0:T(1...) all-reduce(f32[1,1024]{1,0:T(1,128)S(1)} %bitcast.251, ...), channel_id=1, replica_groups=mesh['dp'=16,'tensor'=2] {'dp','tensor'}, use_global_device_ids=true, to_apply=%region_32.33 | all-reduce | flops 12288 | bytes 98304 | tf_op jit(solution)/shard_map/psum | solution.py:237
  965.1 700.4 %all-reduce.9.cloned.1.call-done = (f32[1,1024,3,512]{3,1,2,0:T(8,128)}, f32[1,1024,3,512]{3,1,2,0:T(8,128)}, f32[1,512,1024]{2,1,0:T(8,128)}, f32[1,512,1024]{2...) async-done(((f32[1,1024,3,512]{3,1,2,0:T(8,128)}, f32[1,1024,3,512]{3,1,2,0:T(8,128)}, ...) | async-done | bytes 50331664 | tf_op jit(solution)/shard_map/psum | solution.py:226
  1665.4 13.7 pad_maximum_fusion.1
  1690.8 12.4 pad_maximum_fusion.2
  (287 shorter events, 248.7 us)
Async XLA Ops:
  7.2 43.1 %copy-start = (bf16[1024,3,512]{2,0,1:T(8,128)(2,1)S(1)}, bf16[1024,3,512]{2,0,1:T(8,128)(2,1)}, u32[]{:S(2)}) copy-start(bf16[1024,3,512]{2,0,1:T(8,128)(2,1)} %param.42) | copy-start | bytes 9437188
  7.2 43.1 %all-gather.8.cloned.1.call-start = ((), (), s32[]{:S(2)}) async-start(), calls=%async_computation.7 | async-start | bytes 3145728 | tf_op jit(solution)/shard_map/all_gather | solution.py:133
  14.3 122.9 %reduce-scatter.8.cloned.1.call-start = ((), (), s32[]{:S(2)}) async-start(), calls=%async_computation.8 | async-start | bytes 6291456 | tf_op jit(solution)/shard_map/reduce_scatter | solution.py:148
  78.1 59.1 %copy-start.61 = (f32[1024]{0:T(1024)S(1)}, f32[1024]{0:T(1024)}, u32[]{:S(2)}) copy-start(f32[1024]{0:T(1024)} %param.45) | copy-start | bytes 12292
  82.6 58.6 %copy-start.40 = (f32[1024]{0:T(1024)S(1)}, f32[1024]{0:T(1024)}, u32[]{:S(2)}) copy-start(f32[1024]{0:T(1024)} %param.46) | copy-start | bytes 12292
  82.6 58.6 %copy-start.62 = (f32[1024]{0:T(1024)S(1)}, f32[1024]{0:T(1024)}, u32[]{:S(2)}) copy-start(f32[1024]{0:T(1024)} %param.47) | copy-start | bytes 12292
  82.7 93.9 %all-gather.10.cloned.1.call-start = ((), (), s32[]{:S(2)}) async-start(), calls=%async_computation.9 | async-start | bytes 3145728 | tf_op jit(solution)/shard_map/all_gather | solution.py:152
  143.3 68.3 %all-gather.14.cloned.1.call-start = ((), (), s32[]{:S(2)}) async-start(), calls=%async_computation.13 | async-start | bytes 3145728 | tf_op jit(solution)/shard_map/all_gather | solution.py:165
  145.8 65.9 %copy-start.71 = (f32[2048]{0:T(1024)S(1)}, f32[2048]{0:T(1024)}, u32[]{:S(2)}) copy-start(f32[2048]{0:T(1024)} %param.49) | copy-start | bytes 24580
  145.8 142.3 %reduce-scatter.14.cloned.1.call-start = ((), (), s32[]{:S(2)}) async-start(), calls=%async_computation.14 | async-start | bytes 6291456 | tf_op jit(solution)/shard_map/reduce_scatter | solution.py:180
  233.5 111.7 %reduce-scatter.10.cloned.1.call-start = ((), (), s32[]{:S(2)}) async-start(), calls=%async_computation.10 | async-start | bytes 6291456 | tf_op jit(solution)/shard_map/reduce_scatter | solution.py:160
  245.7 99.5 %copy-start.52 = (f32[1024]{0:T(1024)S(1)}, f32[1024]{0:T(1024)}, u32[]{:S(2)}) copy-start(f32[1024]{0:T(1024)} %param.51) | copy-start | bytes 12292
  245.7 134.7 %all-gather.12.cloned.1.call-start = ((), (), s32[]{:S(2)}) async-start(), calls=%async_computation.11 | async-start | bytes 3145728 | tf_op jit(solution)/shard_map/all_gather | solution.py:152
  246.5 169.2 %all-gather.18.cloned.1.call-start = ((), (), s32[]{:S(2)}) async-start(), calls=%async_computation.17 | async-start | bytes 3145728 | tf_op jit(solution)/shard_map/all_gather | solution.py:165
  350.0 41.3 %copy-start.46 = (f32[512]{0:T(512)}, f32[512]{0:T(512)S(1)}, u32[]{:S(2)}) copy-start(f32[512]{0:T(512)S(1)} %negate_multiply_fusion.3) | copy-start | bytes 6148
  353.8 97.2 %all-gather.16.cloned.1.call-start = ((), (), s32[]{:S(2)}) async-start(), calls=%async_computation.15 | async-start | bytes 3145728 | tf_op jit(solution)/shard_map/all_gather | solution.py:187
  391.3 152.6 %reduce-scatter.18.cloned.1.call-start = ((), (), s32[]{:S(2)}) async-start(), calls=%async_computation.18 | async-start | bytes 6291456 | tf_op jit(solution)/shard_map/reduce_scatter | solution.py:180
  437.6 127.8 %reduce-scatter.12.cloned.1.call-start = ((), (), s32[]{:S(2)}) async-start(), calls=%async_computation.12 | async-start | bytes 6291456 | tf_op jit(solution)/shard_map/reduce_scatter | solution.py:160
  449.6 179.0 %all-gather.20.cloned.1.call-start = ((), (), s32[]{:S(2)}) async-start(), calls=%async_computation.19 | async-start | bytes 3145728 | tf_op jit(solution)/shard_map/all_gather | solution.py:187
  573.5 331.6 %reduce-scatter.16.cloned.1.call-start = ((), (), s32[]{:S(2)}) async-start(), calls=%async_computation.16 | async-start | bytes 6291456 | tf_op jit(solution)/shard_map/reduce_scatter | solution.py:212
  628.3 276.8 %reduce-scatter.20.cloned.1.call-start = ((), (), s32[]{:S(2)}) async-start(), calls=%async_computation.20 | async-start | bytes 6291456 | tf_op jit(solution)/shard_map/reduce_scatter | solution.py:212
  773.9 891.5 %all-reduce.9.cloned.1.call-start = ((), (), s32[]{:S(2)}) async-start(), calls=%async_computation.21 | async-start | bytes 100663296 | tf_op jit(solution)/shard_map/psum | solution.py:226
  785.1 15.9 copy-start.32
  785.1 15.9 copy-start.33
  785.1 15.8 copy-start.34
  830.0 75.2 %copy-start.42 = (f32[512]{0:T(512)S(1)}, f32[512]{0:T(512)}, u32[]{:S(2)}) copy-start(f32[512]{0:T(512)} %copy-done.41) | copy-start | bytes 6148
  830.0 75.2 %copy-start.43 = (f32[1024]{0:T(1024)S(1)}, f32[1024]{0:T(1024)}, u32[]{:S(2)}) copy-start(f32[1024]{0:T(1024)} %param.40) | copy-start | bytes 12292
  830.0 79.1 %copy-start.51 = (f32[512]{0:T(512)S(1)}, f32[512]{0:T(512)}, u32[]{:S(2)}) copy-start(f32[512]{0:T(512)} %copy-done.50) | copy-start | bytes 6148
  830.0 79.1 %copy-start.45 = (f32[512]{0:T(512)S(1)}, f32[512]{0:T(512)}, u32[]{:S(2)}) copy-start(f32[512]{0:T(512)} %copy-done.44) | copy-start | bytes 6148
  832.9 80.8 %copy-start.47 = (f32[512]{0:T(512)S(1)}, f32[512]{0:T(512)}, u32[]{:S(2)}) copy-start(f32[512]{0:T(512)} %copy-done.46) | copy-start | bytes 6148
  832.9 80.8 %copy-start.49 = (f32[512]{0:T(512)S(1)}, f32[512]{0:T(512)}, u32[]{:S(2)}) copy-start(f32[512]{0:T(512)} %copy-done.48) | copy-start | bytes 6148
  1665.4 16.4 copy-start.17
  (61 other events, 412.9 us)
Sparse Core Ops, SparseCore 0:
  14.5 35.8 all-gather.7
  82.8 54.3 reduce-scatter.7
  143.4 33.0 all-gather.9
  178.5 33.0 all-gather.13
  233.6 54.3 reduce-scatter.13
  290.8 54.3 reduce-scatter.9
  347.3 33.0 all-gather.11
  382.5 33.0 all-gather.17
  417.8 33.0 all-gather.15
  453.6 54.3 reduce-scatter.17
  510.9 54.3 reduce-scatter.11
  573.7 33.0 all-gather.19
  628.4 54.3 reduce-scatter.15
  774.0 54.6 reduce-scatter.19
  835.6 829.8 all-reduce.8
where the time goes:
time: 1720 us; the launch traced here: 1710 us
  waiting for transfers between devices  1010 us (59%)
  matrix products  436 us (25%)
  other arithmetic  113 us (7%)
  blocking collectives  104 us (6%)
  local copies, waits for them, and re-layouts  31.4 us (2%)
    psum x1, waiting for transfers between devices, per_device(): lax.psum((weight_part[0], weight_part[1], weight_part[2], weight_part[3],...  700 us
    dot_general x4, matrix products, attend_backward(): jnp.einsum('shqk,sqhe->skhe', grad_scores, query_rows, preferred_element_...  97.2 us
    dot_general x4, matrix products, attend_backward(): jnp.einsum('shqk,skhe->sqhe', grad_scores, key_rows[:, :limit], preferred...  94.5 us
    reduce_scatter x2, waiting for transfers between devices, per_device(): lax.psum_scatter(second_terms, 'tensor', scatter_dimension=0, tiled=True)  71.4 us
    psum x1, blocking collectives, per_device(): lax.psum((weight_part[0], weight_part[1], weight_part[2], weight_part[3],...  65 us
    all_gather x2, waiting for transfers between devices, per_device(): lax.all_gather(normed_two.astype(jnp.bfloat16), 'tensor', axis=0, tiled=T...  56.9 us
    reduce_scatter x1, waiting for transfers between devices, per_device(): lax.psum_scatter(branch_terms, 'tensor', scatter_dimension=0, tiled=True)  54.5 us
    all_gather x2, waiting for transfers between devices, per_device(): grad_second_all = lax.all_gather(grad_second, 'tensor', axis=0, tiled=True)  48.3 us
  transfers between devices with their start and end apart: 15, of which 11 were waited for; matrix products, arithmetic and copies ran while one was open for 27% of the time, Pallas kernels for 0%

commit v1 on v0

v1 whole, which is shorter than its diff:
```python
from functools import partial

import jax
import jax.numpy as jnp
from jax import lax
from jax.experimental import pallas as pl
from jax.experimental.pallas import tpu as pltpu
from jax.sharding import PartitionSpec as P

HEAD = 64
LEN = 1024
DEPTH_A = 12
DEPTH_B = 48
PAIR = 2 * HEAD
BLOCK_Q = 256
bf16 = jnp.bfloat16
f32 = jnp.float32

DOT_NT = (((1,), (1,)), ((), ()))
DOT_NN = (((1,), (0,)), ((), ()))
DOT_TN = (((0,), (0,)), ((), ()))


def dot(left, right, dims):
    return lax.dot_general(left, right, dims, preferred_element_type=f32)


def head_rows(rows, head):
    lane = lax.broadcasted_iota(jnp.int32, rows.shape, 1)
    return jnp.where((lane // HEAD) == head, rows, jnp.zeros_like(rows))


def scores_of(key_ref, query_rows, lo, hi):
    diag = dot(key_ref[lo:hi, :], query_rows, DOT_NT)
    key_pos = lax.broadcasted_iota(jnp.int32, diag.shape, 0)
    query_pos = lax.broadcasted_iota(jnp.int32, diag.shape, 1)
    diag = jnp.where(key_pos <= query_pos, diag, -1e30)
    if lo == 0:
        return diag
    return jnp.concatenate([dot(key_ref[:lo, :], query_rows, DOT_NT), diag], axis=0)


def attend_forward_kernel(q_ref, k_ref, v_ref, o_ref, lse_ref, vt_ref):
    vt_ref[...] = v_ref[...].astype(f32).T.astype(bf16)
    for index in range(LEN // BLOCK_Q):
        lo, hi = index * BLOCK_Q, (index + 1) * BLOCK_Q
        query_rows = q_ref[lo:hi, :] * jnp.asarray(0.125, bf16)
        mixed = []
        for head in range(2):
            scores = scores_of(k_ref, head_rows(query_rows, head), lo, hi)
            highest = jnp.max(scores, axis=0, keepdims=True)
            raised = jnp.exp(scores - highest)
            totals = jnp.sum(raised, axis=0, keepdims=True)
            probabilities = (raised * (1.0 / totals)).astype(bf16)
            mixed.append(dot(vt_ref[head * HEAD : (head + 1) * HEAD, :hi], probabilities, DOT_NN))
            lse_ref[0, head : head + 1, lo:hi] = highest + jnp.log(totals)
        o_ref[lo:hi, :] = jnp.concatenate(mixed, axis=0).T.astype(bf16)


def attend_backward_kernel(q_ref, k_ref, v_ref, lse_ref, do_ref, dq_ref, dk_ref, dv_ref, kt_ref, dk_acc, dv_acc):
    kt_ref[...] = k_ref[...].astype(f32).T.astype(bf16)
    blocks = LEN // BLOCK_Q
    for index in reversed(range(blocks)):
        lo, hi = index * BLOCK_Q, (index + 1) * BLOCK_Q
        query_rows = q_ref[lo:hi, :] * jnp.asarray(0.125, bf16)
        grad_rows = do_ref[lo:hi, :]
        probs, grads, queries, douts, dqs = [], [], [], [], []
        for head in range(2):
            query_head = head_rows(query_rows, head)
            grad_head = head_rows(grad_rows, head)
            scores = scores_of(k_ref, query_head, lo, hi)
            probabilities = jnp.exp(scores - lse_ref[0, head : head + 1, lo:hi])
            grad_probs = dot(v_ref[:hi, :], grad_head, DOT_NT)
            centre = jnp.sum(probabilities * grad_probs, axis=0, keepdims=True)
            grad_scores = (probabilities * (grad_probs - centre)).astype(bf16)
            dqs.append(dot(kt_ref[head * HEAD : (head + 1) * HEAD, :hi], grad_scores, DOT_NN))
            probs.append(probabilities.astype(bf16))
            grads.append(grad_scores)
            queries.append(query_head)
            douts.append(grad_head)
        dq_ref[lo:hi, :] = (0.125 * jnp.concatenate(dqs, axis=0).T).astype(bf16)
        dk = dot(jnp.concatenate(grads, axis=1), jnp.concatenate(queries, axis=0), DOT_NN)
        dv = dot(jnp.concatenate(probs, axis=1), jnp.concatenate(douts, axis=0), DOT_NN)
        if index == blocks - 1:
            dk_acc[...] = dk
            dv_acc[...] = dv
        else:
            dk_acc[:hi, :] = dk_acc[:hi, :] + dk
            dv_acc[:hi, :] = dv_acc[:hi, :] + dv
    dk_ref[...] = dk_acc[...].astype(bf16)
    dv_ref[...] = dv_acc[...].astype(bf16)


def attend_forward(queries, key_rows, value_rows):
    rows, cols = queries.shape
    seqs, pairs = rows // LEN, cols // PAIR
    spec = pl.BlockSpec((LEN, PAIR), lambda s, p: (s, p))
    return pl.pallas_call(
        attend_forward_kernel,
        grid=(seqs, pairs),
        in_specs=[spec] * 3,
        out_specs=[spec, pl.BlockSpec((1, 2, LEN), lambda s, p: (s * pairs + p, 0, 0))],
        out_shape=[
            jax.ShapeDtypeStruct((rows, cols), bf16),
            jax.ShapeDtypeStruct((seqs * pairs, 2, LEN), f32),
        ],
        scratch_shapes=[pltpu.VMEM((PAIR, LEN), bf16)],
        name="attend_forward",
    )(queries, key_rows, value_rows)


def attend_backward(queries, key_rows, value_rows, log_totals, grad_mixed):
    rows, cols = queries.shape
    seqs, pairs = rows // LEN, cols // PAIR
    spec = pl.BlockSpec((LEN, PAIR), lambda s, p: (s, p))
    lse_spec = pl.BlockSpec((1, 2, LEN), lambda s, p: (s * pairs + p, 0, 0))
    return pl.pallas_call(
        attend_backward_kernel,
        grid=(seqs, pairs),
        in_specs=[spec, spec, spec, lse_spec, spec],
        out_specs=[spec] * 3,
        out_shape=[jax.ShapeDtypeStruct((rows, cols), bf16)] * 3,
        scratch_shapes=[
            pltpu.VMEM((PAIR, LEN), bf16),
            pltpu.VMEM((LEN, PAIR), f32),
            pltpu.VMEM((LEN, PAIR), f32),
        ],
        name="attend_backward",
    )(queries, key_rows, value_rows, log_totals, grad_mixed)


GELU_C = 0.7978845608028654


def hidden_kernel(scale_a, ha_ref, hb_ref, dz_ref, wfc_ref, bias_ref, wproj_ref, fa_ref, fb_ref, dua_ref, dub_ref, sa_ref, sb_ref):
    grad_active = dot(dz_ref[...], wproj_ref[...], DOT_NT)
    for h_ref, f_ref, du_ref, s_ref, scale in (
        (ha_ref, fa_ref, dua_ref, sa_ref, scale_a),
        (hb_ref, fb_ref, dub_ref, sb_ref, 1.0),
    ):
        hidden = dot(h_ref[...], wfc_ref[...], DOT_NN) + bias_ref[...]
        square = hidden * hidden
        bend = jnp.tanh(GELU_C * (hidden + 0.044715 * (hidden * square)))
        cdf = 0.5 * (1.0 + bend)
        f_ref[...] = (hidden * cdf).astype(bf16)
        slope = cdf + hidden * (0.5 * (1.0 - bend * bend)) * (
            GELU_C * (1.0 + (3 * 0.044715) * square)
        )
        grad = ((scale * grad_active) * slope).astype(bf16)
        du_ref[...] = grad
        s_ref[0] = jnp.sum(grad.astype(f32), axis=0, keepdims=True)


def hidden_layer(scale_a, h_a, h_b, dz, w_fc, fc_bias, w_proj):
    rows, width = h_a.shape
    hidden = w_fc.shape[1]
    tile_r = min(512, rows)
    tile_c = min(512, hidden)
    row_spec = pl.BlockSpec((tile_r, width), lambda r, c: (r, 0))
    out_spec = pl.BlockSpec((tile_r, tile_c), lambda r, c: (r, c))
    sum_spec = pl.BlockSpec((1, 1, tile_c), lambda r, c: (r, 0, c))
    out = jax.ShapeDtypeStruct((rows, hidden), bf16)
    sums = jax.ShapeDtypeStruct((rows // tile_r, 1, hidden), f32)
    return pl.pallas_call(
        partial(hidden_kernel, scale_a),
        grid=(rows // tile_r, hidden // tile_c),
        in_specs=[
            row_spec,
            row_spec,
            row_spec,
            pl.BlockSpec((width, tile_c), lambda r, c: (0, c)),
            pl.BlockSpec((1, tile_c), lambda r, c: (0, c)),
            pl.BlockSpec((tile_c, width), lambda r, c: (c, 0)),
        ],
        out_specs=[out_spec] * 4 + [sum_spec] * 2,
        out_shape=[out] * 4 + [sums] * 2,
        name="hidden_layer",
    )(h_a, h_b, dz, w_fc, fc_bias.reshape(1, hidden), w_proj)


def norm_parts(values):
    centre = values - jnp.mean(values, axis=-1, keepdims=True)
    spread = jnp.mean(centre * centre, axis=-1, keepdims=True)
    inverse = lax.rsqrt(spread + 1e-05)
    return centre * inverse, inverse


def norm_back(unit, inverse, gain, grad):
    scaled = grad * gain
    along = jnp.mean(scaled * unit, axis=-1, keepdims=True)
    return inverse * (scaled - jnp.mean(scaled, axis=-1, keepdims=True) - unit * along)


def solution(mesh):
    tensor = mesh.shape["tensor"]
    devices_dp = mesh.shape["dp"]
    swap = [(0, 1), (1, 0)]

    def own_rows(values, rows, other=False):
        place = lax.axis_index("tensor")
        if other:
            place = 1 - place
        return lax.dynamic_slice_in_dim(values, place * rows, rows, axis=0)

    def gather_rows(values):
        if tensor != 2:
            return lax.all_gather(values, "tensor", axis=0, tiled=True)
        there = lax.ppermute(values, "tensor", swap)
        first = lax.axis_index("tensor") == 0
        return jnp.concatenate(
            [jnp.where(first, values, there), jnp.where(first, there, values)], axis=0
        )

    def total_rows(shares):
        if tensor != 2:
            return lax.psum(shares.astype(bf16), "tensor").astype(f32)
        there = lax.ppermute(shares.astype(bf16), "tensor", swap)
        return shares + there.astype(f32)

    def scatter_rows(shares, rows):
        if tensor != 2:
            low = shares.astype(bf16)
            return lax.psum_scatter(low, "tensor", scatter_dimension=0, tiled=True).astype(f32)
        low = shares.astype(bf16)
        there = lax.ppermute(own_rows(low, rows, other=True), "tensor", swap)
        return own_rows(low, rows).astype(f32) + there.astype(f32)

    def reduce_dp(share):
        shape = share.shape
        flat = share.astype(bf16).reshape(shape[0], -1)
        part = lax.psum_scatter(flat, "dp", scatter_dimension=0, tiled=True)
        return lax.all_gather(part, "dp", axis=0, tiled=True).reshape(shape)

    def per_device(
        tokens,
        cotangent,
        gain_one,
        bias_one,
        w_qkv,
        bias_qv,
        w_out,
        out_bias,
        gain_two,
        bias_two,
        w_fc,
        fc_bias,
        w_proj,
        proj_bias,
    ):
        own, width = tokens.shape
        rows = own * tensor
        cols = w_qkv.shape[2]
        hidden_cols = w_fc.shape[1]
        scale_a = float(DEPTH_A) ** (-0.5)
        scale_b = float(DEPTH_B) ** (-0.5)
        factor = 2.0
        assert scale_a == factor * scale_b

        residual = gather_rows(tokens).astype(f32)
        upstream_low = gather_rows(cotangent)
        upstream = upstream_low.astype(f32)
        unit_one, inverse_one = norm_parts(residual)
        normed = (unit_one * gain_one + bias_one).astype(bf16)
        flat_w = w_qkv.reshape(width, 3 * cols)
        projected = dot(normed, flat_w, DOT_NN)
        queries = (projected[:, :cols] + bias_qv[0]).astype(bf16)
        key_rows = projected[:, cols : 2 * cols].astype(bf16)
        value_rows = (projected[:, 2 * cols :] + bias_qv[1]).astype(bf16)
        mixed, log_totals = attend_forward(queries, key_rows, value_rows)
        branch = total_rows(dot(mixed, w_out, DOT_NN)) + out_bias

        dz = (scale_b * upstream).astype(bf16)
        dz_own = (scale_b * cotangent.astype(f32)).astype(bf16)
        proj_sum = jnp.sum(dz_own.astype(f32), axis=0)

        middles, units, inverses, normed_two = [], [], [], []
        for scale in (scale_a, scale_b):
            middle = residual + scale * branch
            unit, inverse = norm_parts(middle)
            middles.append(middle)
            units.append(unit)
            inverses.append(inverse)
            normed_two.append((unit * gain_two + bias_two).astype(bf16))
        f_a, f_b, du_a, du_b, sum_a, sum_b = hidden_layer(
            factor, normed_two[0], normed_two[1], dz, w_fc, fc_bias, w_proj
        )

        outputs, grad_tokens, vectors, weights = [], [], [], []
        place = lax.axis_index("tensor")
        for depth, (scale, active, grad_hidden, hidden_sum, times) in enumerate(
            ((scale_a, f_a, du_a, sum_a, factor), (scale_b, f_b, du_b, sum_b, 1.0))
        ):
            grad_two = total_rows(dot(grad_hidden, w_fc, DOT_NT))
            grad_w_proj = reduce_dp(times * dot(active, dz, DOT_TN))
            grad_w_fc = reduce_dp(dot(normed_two[depth], grad_hidden, DOT_TN))
            second = scatter_rows(dot(active, w_proj, DOT_NN), own) + proj_bias
            outputs.append((own_rows(middles[depth], own) + scale * second).astype(bf16))

            grad_middle = upstream + norm_back(units[depth], inverses[depth], gain_two, grad_two)
            grad_branch = (scale * grad_middle).astype(bf16)
            own_grad_two = own_rows(grad_two, own)
            grad_gain_two = jnp.sum(own_grad_two * own_rows(units[depth], own), axis=0)
            grad_bias_two = jnp.sum(own_grad_two, axis=0)
            grad_out_bias = jnp.sum(own_rows(grad_branch, own).astype(f32), axis=0)

            grad_w_out = reduce_dp(dot(mixed, grad_branch, DOT_TN))
            grad_mixed = dot(grad_branch, w_out, DOT_NT).astype(bf16)
            dq, dk, dv = attend_backward(queries, key_rows, value_rows, log_totals, grad_mixed)
            stacked = jnp.concatenate([dq, dk, dv], axis=1)
            grad_bias_qv = jnp.stack(
                [jnp.sum(dq.astype(f32), axis=0), jnp.sum(dv.astype(f32), axis=0)]
            )
            grad_w_qkv = reduce_dp(dot(normed, stacked, DOT_TN))
            grad_one_share = dot(stacked, flat_w, DOT_NT)
            grad_gain_one = jnp.sum(grad_one_share * unit_one, axis=0)
            grad_bias_one = jnp.sum(grad_one_share, axis=0)
            grad_one = scatter_rows(grad_one_share, own)
            grad_tokens.append(
                own_rows(grad_middle, own)
                + norm_back(
                    own_rows(unit_one, own), own_rows(inverse_one, own), gain_one, grad_one
                )
            )
            weights.append((grad_w_qkv, grad_w_out, grad_w_fc, grad_w_proj))
            slots = jnp.concatenate(
                [jnp.sum(hidden_sum, axis=(0, 1)), grad_bias_qv[0], grad_bias_qv[1]]
            )
            spread_slots = jnp.where(
                jnp.arange(tensor)[:, None] == place, slots[None, :], 0.0
            ).reshape(-1)
            vectors.append(
                jnp.concatenate(
                    [
                        grad_gain_one,
                        grad_bias_one,
                        grad_out_bias,
                        grad_gain_two,
                        grad_bias_two,
                        times * proj_sum,
                        spread_slots,
                    ]
                )
            )

        summed = lax.psum(jnp.stack(vectors), ("dp", "tensor"))
        small = [summed[:, index * width : (index + 1) * width] for index in range(6)]
        slot_len = hidden_cols + 2 * cols
        mine = lax.dynamic_slice_in_dim(summed, 6 * width + place * slot_len, slot_len, axis=1)
        grad_fc_bias = mine[:, :hidden_cols]
        grad_bias_qv = mine[:, hidden_cols:].reshape(2, 2, cols)
        stack = [
            jnp.stack([weights[0][index].astype(f32), weights[1][index].astype(f32)])
            for index in range(4)
        ]
        return (
            jnp.stack(outputs),
            jnp.stack(grad_tokens),
            small[0],
            small[1],
            stack[0].reshape(2, width, 3, cols),
            grad_bias_qv,
            stack[1],
            small[2],
            small[3],
            small[4],
            stack[2],
            grad_fc_bias,
            stack[3],
            small[5],
        )

    return jax.shard_map(
        per_device,
        mesh=mesh,
        in_specs=(
            P(("dp", "tensor"), None),
            P(("dp", "tensor"), None),
            P(),
            P(),
            P(None, None, "tensor"),
            P(None, "tensor"),
            P("tensor", None),
            P(),
            P(),
            P(),
            P(None, "tensor"),
            P("tensor"),
            P("tensor", None),
            P(),
        ),
        out_specs=(
            P(None, ("dp", "tensor"), None),
            P(None, ("dp", "tensor"), None),
            P(),
            P(),
            P(None, None, None, "tensor"),
            P(None, None, "tensor"),
            P(None, "tensor", None),
            P(),
            P(),
            P(),
            P(None, None, "tensor"),
            P(None, "tensor"),
            P(None, "tensor", None),
            P(),
        ),
        check_vma=False,
    )
```

time: 1720 us -> 1260 us (0.73)
  matrix products: 436 us -> 107 us
  waiting for transfers between devices: 1010 us -> 874 us
  blocking collectives: 104 us -> 0 us
  Pallas kernels: 0 us -> 97.4 us
  local copies, waits for them, and re-layouts: 31.4 us -> 52.2 us
  other arithmetic: 113 us -> 95.6 us
    psum x1, waiting for transfers between devices: 700 us -> 0.01 us  [per_device(): summed = lax.psum(jnp.stack(vectors), ('dp', 'tensor'))]
    dot_general x42 -> x18, matrix products: 436 us -> 107 us  [dot(): return lax.dot_general(left, right, dims, preferred_element_type=f32)]
    reduce_scatter x7 -> x8, waiting for transfers between devices: 167 us -> 412 us  [reduce_dp(): part = lax.psum_scatter(flat, 'dp', scatter_dimension=0, tiled=True)]
    ppermute x0 -> x9, waiting for transfers between devices: none -> 241 us  [the longest x3 132 us: total_rows(): there = lax.ppermute(shares.astype(bf16), 'tensor', swap)]
    psum x2 -> x0, blocking collectives: 104 us -> none  [the longest x1 65 us: per_device(): lax.psum((weight_part[0], weight_part[1], weight_part[2], weight_part[3],...]
    pallas_call x0 -> x4, Pallas kernels: none -> 97.4 us  [the longest x2 48.9 us: attend_backward(): pl.pallas_call(attend_backward_kernel, grid=(seqs, pairs), in_specs=[spec...]
    all_gather x7 -> x8, waiting for transfers between devices: 140 us -> 220 us  [reduce_dp(): return lax.all_gather(part, 'dp', axis=0, tiled=True).reshape(shape)]
    reduce_sum x19 -> x18, other arithmetic: 51.2 us -> 26.5 us  [the longest x1 4.96 us: norm_back(): jnp.mean(scaled, axis=-1, keepdims=True)]
  transfers between devices with their start and end apart: 15 -> 26, of which waited for: 11 -> 21; matrix products, arithmetic and copies ran while one was open for 27% -> 14% of each run, Pallas kernels for 0% -> 4%
where the time goes in v1:
time: 1260 us
  waiting for transfers between devices  874 us (69%)
  matrix products  107 us (8%)
  Pallas kernels  97.4 us (8%)
  other arithmetic  95.6 us (8%)
  local copies, waits for them, and re-layouts  52.2 us (4%)
  between operations  16.4 us (1%)
    reduce_scatter x8, waiting for transfers between devices, reduce_dp(): part = lax.psum_scatter(flat, 'dp', scatter_dimension=0, tiled=True)  412 us
    all_gather x8, waiting for transfers between devices, reduce_dp(): return lax.all_gather(part, 'dp', axis=0, tiled=True).reshape(shape)  220 us
    ppermute x3, waiting for transfers between devices, total_rows(): there = lax.ppermute(shares.astype(bf16), 'tensor', swap)  132 us
    dot_general x18, matrix products, dot(): return lax.dot_general(left, right, dims, preferred_element_type=f32)  107 us
    ppermute x4, waiting for transfers between devices, scatter_rows(): there = lax.ppermute(own_rows(low, rows, other=True), 'tensor', swap)  69 us
    pallas_call x2, Pallas kernels, attend_backward(): pl.pallas_call(attend_backward_kernel, grid=(seqs, pairs), in_specs=[spec...  48.9 us
    ppermute x2, waiting for transfers between devices, gather_rows(): there = lax.ppermute(values, 'tensor', swap)  40.3 us
    unnamed x106, local copies, waits for them, and re-layouts  33.8 us
  transfers between devices with their start and end apart: 26, of which 21 were waited for; matrix products, arithmetic and copies ran while one was open for 14% of the time, Pallas kernels for 4%

profile of v1, /device:TPU:0, one launch (start us, length us, event | category | flops | bytes accessed | tf_op | source)
XLA Modules:
  0.0 1255.3 jit_solution(15842645488960915116)
XLA Ops:
  15.9 19.5 %collective-permute-done = bf16[512,1024]{1,0:T(8,128)(2,1)S(1)} collective-permute-done((bf16[512,1024]{1,0:T(8,128)(2,1)}, bf16[512,1024]{1,0:T(8,128)(2,1)S(1)}, u32[]{:S(2)}, u32[]{:S(2)}) %collective-permute-start) | collective-permute-done | bytes 1048608 | tf_op jit(solution)/shard_map/ppermute | solution.py:208
  36.3 20.8 %collective-permute-done.2 = bf16[512,1024]{1,0:T(8,128)(2,1)} collective-permute-done((bf16[512,1024]{1,0:T(8,128)(2,1)}, bf16[512,1024]{1,0:T(8,128)(2,1)}, u32[]{:S(2)}, u32[]{:S(2)}) %collective-permute-start.2) | collective-permute-done | bytes 1048608 | tf_op jit(solution)/shard_map/ppermute | solution.py:208
  69.4 18.4 %attend_forward.1 = (bf16[1024,512]{1,0:T(8,128)(2,1)}, f32[4,2,1024]{2,1,0:T(2,128)}) custom-call(bf16[1024,512]{1,0:T(8,128)(2,1)} %get-tuple-element.91.q_ref, bf16[1024,512]{1,0:T(8,128)(2,1)} %slice.69.k_ref, bf16[1024,512]{1,0:T(8,128)(2,1)} %get-tuple-element.90.v_ref), custom_call_target="tpu_custom_call" | custom-call | tf_op jit(solution)/shard_map/attend_forward/pallas_call | solution.py:98
  94.2 43.2 %collective-permute-done.1 = bf16[1024,1024]{1,0:T(8,128)(2,1)S(1)} collective-permute-done((bf16[1024,1024]{1,0:T(8,128)(2,1)S(1)}, bf16[1024,1024]{1,0:T(8,128)(2,1)S(1)}, u32[]{:S(2)}, u32[]{:S(2)}) %collective-permute-start.1) | collective-permute-done | bytes 2097184 | tf_op jit(solution)/shard_map/ppermute | solution.py:217
  148.1 30.1 %hidden_layer.1 = (bf16[1024,2048]{1,0:T(8,128)(2,1)}, bf16[1024,2048]{1,0:T(8,128)(2,1)}, bf16[1024,2048]{1,0:T(8,128)(2,1)}, bf16[1024,2048]{1,0:T(8,128)(2,1)...) custom-call(bf16[1024,1024]{1,0:T(8,128)(2,1)} %get-tuple-element.113.ha_ref, ...), custom_call_target="tpu_custom_call" | custom-call | tf_op jit(solution)/shard_map/hidden_layer/pallas_call | solution.py:164
  194.3 46.5 %collective-permute-done.5 = bf16[1024,1024]{1,0:T(8,128)(2,1)S(1)} collective-permute-done((bf16[1024,1024]{1,0:T(8,128)(2,1)S(1)}, bf16[1024,1024]{1,0:T(8,128)(2,1)S(1)}, u32[]{:S(2)}, u32[]{:S(2)}) %collective-permute-start.5) | collective-permute-done | bytes 2097184 | tf_op jit(solution)/shard_map/ppermute | solution.py:217
  240.8 42.3 %collective-permute-done.7 = bf16[1024,1024]{1,0:T(8,128)(2,1)S(1)} collective-permute-done((bf16[1024,1024]{1,0:T(8,128)(2,1)S(1)}, bf16[1024,1024]{1,0:T(8,128)(2,1)S(1)}, u32[]{:S(2)}, u32[]{:S(2)}) %collective-permute-start.7) | collective-permute-done | bytes 2097184 | tf_op jit(solution)/shard_map/ppermute | solution.py:217
  310.9 24.4 %attend_backward.3 = (bf16[1024,512]{1,0:T(8,128)(2,1)}, bf16[1024,512]{1,0:T(8,128)(2,1)}, bf16[1024,512]{1,0:T(8,128)(2,1)}) custom-call(bf16[1024,512]{1,0:T(8,128)(2,1)} %get-tuple-element.91.q_ref, bf16[1024,512]{1,0:T(8,128)(2,1)} %slice.69.k_ref, bf16[1024,512]{1,0:T(8,128)(2,1)} %get-tuple-element.90.v_ref, f32[4,2,1024]{2,1,0:T(2,128)} %get-tuple-element.32.lse_ref, ...), custom_call_target="tpu_custom_call" | custom-call | tf_op jit(solution)/shard_map/attend_backward/pallas_call | solution.py:117
  348.8 24.5 %attend_backward.2 = (bf16[1024,512]{1,0:T(8,128)(2,1)}, bf16[1024,512]{1,0:T(8,128)(2,1)}, bf16[1024,512]{1,0:T(8,128)(2,1)}) custom-call(bf16[1024,512]{1,0:T(8,128)(2,1)} %get-tuple-element.91.q_ref, bf16[1024,512]{1,0:T(8,128)(2,1)} %slice.69.k_ref, bf16[1024,512]{1,0:T(8,128)(2,1)} %get-tuple-element.90.v_ref, f32[4,2,1024]{2,1,0:T(2,128)} %get-tuple-element.32.lse_ref, ...), custom_call_target="tpu_custom_call" | custom-call | tf_op jit(solution)/shard_map/attend_backward/pallas_call | solution.py:117
  383.1 9.4 convolution_convert_fusion.4
  392.7 9.4 convolution_convert_fusion.3
  403.4 9.1 multiply_convert_fusion
  412.9 9.1 convolution_convert_fusion.2
  450.7 40.0 %reduce-scatter.11.cloned.1.call-done = bf16[64,1536]{1,0:T(8,128)(2,1)} async-done(((bf16[1024,1536]{1,0:T(8,128)(2,1)}), bf16[64,1536]{1,0:T(8,128)(2,1)}) %reduce-scatter.11.cloned.1.call-update) | async-done | bytes 196624 | tf_op jit(solution)/shard_map/reduce_scatter | solution.py:231
  490.8 69.0 %reduce-scatter.9.cloned.1.call-done = bf16[64,1536]{1,0:T(8,128)(2,1)} async-done(((bf16[1024,1536]{1,0:T(8,128)(2,1)}), bf16[64,1536]{1,0:T(8,128)(2,1)}) %reduce-scatter.9.cloned.1.call-update) | async-done | bytes 196624 | tf_op jit(solution)/shard_map/reduce_scatter | solution.py:231
  559.8 75.3 %reduce-scatter.17.cloned.1.call-done = bf16[64,2048]{1,0:T(8,128)(2,1)} async-done(((bf16[1024,2048]{1,0:T(8,128)(2,1)}), bf16[64,2048]{1,0:T(8,128)(2,1)}) %reduce-scatter.17.cloned.1.call-update) | async-done | bytes 262160 | tf_op jit(solution)/shard_map/reduce_scatter | solution.py:231
  635.2 76.1 %reduce-scatter.19.cloned.1.call-done = bf16[64,2048]{1,0:T(8,128)(2,1)} async-done(((bf16[1024,2048]{1,0:T(8,128)(2,1)}), bf16[64,2048]{1,0:T(8,128)(2,1)}) %reduce-scatter.19.cloned.1.call-update) | async-done | bytes 262160 | tf_op jit(solution)/shard_map/reduce_scatter | solution.py:231
  711.4 75.6 %reduce-scatter.21.cloned.1.call-done = bf16[128,1024]{1,0:T(8,128)(2,1)} async-done(((bf16[2048,1024]{1,0:T(8,128)(2,1)}), bf16[128,1024]{1,0:T(8,128)(2,1)}) %reduce-scatter.21.cloned.1.call-update) | async-done | bytes 262160 | tf_op jit(solution)/shard_map/reduce_scatter | solution.py:231
  787.3 75.5 %reduce-scatter.23.cloned.1.call-done = bf16[128,1024]{1,0:T(8,128)(2,1)} async-done(((bf16[2048,1024]{1,0:T(8,128)(2,1)}), bf16[128,1024]{1,0:T(8,128)(2,1)}) %reduce-scatter.23.cloned.1.call-update) | async-done | bytes 262160 | tf_op jit(solution)/shard_map/reduce_scatter | solution.py:231
  884.4 14.0 %collective-permute-done.3 = bf16[512,1024]{1,0:T(8,128)(2,1)} collective-permute-done((bf16[512,1024]{1,0:T(8,128)(2,1)}, bf16[512,1024]{1,0:T(8,128)(2,1)}, u32[]{:S(2)}, u32[]{:S(2)}) %collective-permute-start.3) | collective-permute-done | bytes 1048608 | tf_op jit(solution)/shard_map/ppermute | solution.py:225
  898.3 22.5 %collective-permute-done.4 = bf16[512,1024]{1,0:T(8,128)(2,1)} collective-permute-done((bf16[512,1024]{1,0:T(8,128)(2,1)}, bf16[512,1024]{1,0:T(8,128)(2,1)}, u32[]{:S(2)}, u32[]{:S(2)}) %collective-permute-start.4) | collective-permute-done | bytes 1048608 | tf_op jit(solution)/shard_map/ppermute | solution.py:225
  930.5 12.7 %collective-permute-done.8 = bf16[512,1024]{1,0:T(8,128)(2,1)S(1)} collective-permute-done((bf16[512,1024]{1,0:T(8,128)(2,1)}, bf16[512,1024]{1,0:T(8,128)(2,1)S(1)}, u32[]{:S(2)}, u32[]{:S(2)}) %collective-permute-start.8) | collective-permute-done | bytes 1048608 | tf_op jit(solution)/shard_map/ppermute | solution.py:225
  943.2 19.9 %collective-permute-done.6 = bf16[512,1024]{1,0:T(8,128)(2,1)} collective-permute-done((bf16[512,1024]{1,0:T(8,128)(2,1)}, bf16[512,1024]{1,0:T(8,128)(2,1)}, u32[]{:S(2)}, u32[]{:S(2)}) %collective-permute-start.6) | collective-permute-done | bytes 1048608 | tf_op jit(solution)/shard_map/ppermute | solution.py:225
  976.4 11.0 all-gather.11.cloned.1.call-done
  992.0 41.4 %all-gather.9.cloned.1.call-done = bf16[1024,1536]{1,0:T(8,128)(2,1)} async-done(((bf16[64,1536]{1,0:T(8,128)(2,1)}), bf16[1024,1536]{1,0:T(8,128)(2,1)}) %all-gather.9.cloned.1.call-update) | async-done | bytes 3145744 | tf_op jit(solution)/shard_map/all_gather | solution.py:232
  1046.5 12.6 %copy.37 = f32[2,1024,3,512]{3,1,2,0:T(8,128)} copy(f32[2,1024,3,512]{1,3,2,0:T(8,128)} %maximum_convert_fusion.2) | data formatting | bytes 25165824
  1059.1 25.2 %all-gather.17.cloned.1.call-done = bf16[1024,2048]{1,0:T(8,128)(2,1)} async-done(((bf16[64,2048]{1,0:T(8,128)(2,1)}), bf16[1024,2048]{1,0:T(8,128)(2,1)}) %all-gather.17.cloned.1.call-update) | async-done | bytes 4194320 | tf_op jit(solution)/shard_map/all_gather | solution.py:232
  1084.3 51.0 %all-gather.19.cloned.1.call-done = bf16[1024,2048]{1,0:T(8,128)(2,1)} async-done(((bf16[64,2048]{1,0:T(8,128)(2,1)}), bf16[1024,2048]{1,0:T(8,128)(2,1)}) %all-gather.19.cloned.1.call-update) | async-done | bytes 4194320 | tf_op jit(solution)/shard_map/all_gather | solution.py:232
  1135.3 10.7 maximum_convert_fusion
  1146.0 40.2 %all-gather.21.cloned.1.call-done = bf16[2048,1024]{1,0:T(8,128)(2,1)} async-done(((bf16[128,1024]{1,0:T(8,128)(2,1)}), bf16[2048,1024]{1,0:T(8,128)(2,1)}) %all-gather.21.cloned.1.call-update) | async-done | bytes 4194320 | tf_op jit(solution)/shard_map/all_gather | solution.py:232
  1186.2 51.0 %all-gather.23.cloned.1.call-done = bf16[2048,1024]{1,0:T(8,128)(2,1)} async-done(((bf16[128,1024]{1,0:T(8,128)(2,1)}), bf16[2048,1024]{1,0:T(8,128)(2,1)}) %all-gather.23.cloned.1.call-update) | async-done | bytes 4194320 | tf_op jit(solution)/shard_map/all_gather | solution.py:232
  1237.2 10.8 maximum_convert_fusion.1
  (232 shorter events, 198.0 us)
Async XLA Ops:
  8.0 79.8 %copy-start = (bf16[512,1024]{1,0:T(8,128)(2,1)S(1)}, bf16[512,1024]{1,0:T(8,128)(2,1)}, u32[]{:S(2)}) copy-start(bf16[512,1024]{1,0:T(8,128)(2,1)} %param.20) | copy-start | bytes 3145732
  8.0 441.3 %reduce-scatter.15.cloned.1.call-start = ((), (), s32[]{:S(2)}) async-start(), calls=%async_computation.15 | async-start | bytes 1114112 | tf_op jit(solution)/shard_map/reduce_scatter | solution.py:231
  8.1 27.3 %collective-permute-start = (bf16[512,1024]{1,0:T(8,128)(2,1)}, bf16[512,1024]{1,0:T(8,128)(2,1)S(1)}, u32[]{:S(2)}, u32[]{:S(2)}) collective-permute-start(bf16[512,1024]{1,0:T(8,128)(2,1)} %param.14), channel_id=1, source_target_pairs={{0,1},{1,0},{2,3},{3,2},{4,5},{5,4},{6,7},{7,6},{8,9},{9,8},{10,11... | collective-permute-start | bytes 3145736 | tf_op jit(solution)/shard_map/ppermute | solution.py:208
  11.1 45.9 %collective-permute-start.2 = (bf16[512,1024]{1,0:T(8,128)(2,1)}, bf16[512,1024]{1,0:T(8,128)(2,1)}, u32[]{:S(2)}, u32[]{:S(2)}) collective-permute-start(bf16[512,1024]{1,0:T(8,128)(2,1)} %param.15), channel_id=1, source_target_pairs={{0,1},{1,0},{2,3},{3,2},{4,5},{5,4},{6,7},{7,6},{8,9},{9,8},{10,11... | collective-permute-start | bytes 3145736 | tf_op jit(solution)/shard_map/ppermute | solution.py:208
  90.5 46.9 %copy-start.38 = (f32[1024]{0:T(1024)S(1)}, f32[1024]{0:T(1024)}, u32[]{:S(2)}) copy-start(f32[1024]{0:T(1024)} %param.21) | copy-start | bytes 12292
  90.5 46.8 %collective-permute-start.1 = (bf16[1024,1024]{1,0:T(8,128)(2,1)S(1)}, bf16[1024,1024]{1,0:T(8,128)(2,1)S(1)}, u32[]{:S(2)}, u32[]{:S(2)}) collective-permute-start(bf16[1024,1024]{1,0:T(8,128)(2,1)S(1)} %get-tuple-element.123), channel_id=1, source_target_pairs={{0,1},{1,0},{2,3},{3,2},{4,5},{5,4},{6,7},{7,6},{8,9},{9,8},{10,11... | collective-permute-start | bytes 6291464 | tf_op jit(solution)/shard_map/ppermute | solution.py:217
  186.0 98.4 %copy-start.2 = (f32[1024,1024]{1,0:T(8,128)S(1)}, f32[1024,1024]{1,0:T(8,128)}, u32[]{:S(2)}) copy-start(f32[1024,1024]{1,0:T(8,128)} %get-tuple-element.81) | copy-start | bytes 12582916
  186.0 98.4 %copy-start.4 = (f32[1024,1024]{1,0:T(8,128)S(1)}, f32[1024,1024]{1,0:T(8,128)}, u32[]{:S(2)}) copy-start(f32[1024,1024]{1,0:T(8,128)} %get-tuple-element.114) | copy-start | bytes 12582916
  192.3 48.5 %collective-permute-start.5 = (bf16[1024,1024]{1,0:T(8,128)(2,1)S(1)}, bf16[1024,1024]{1,0:T(8,128)(2,1)S(1)}, u32[]{:S(2)}, u32[]{:S(2)}) collective-permute-start(bf16[1024,1024]{1,0:T(8,128)(2,1)S(1)} %get-tuple-element.125), channel_id=1, source_target_pairs={{0,1},{1,0},{2,3},{3,2},{4,5},{5,4},{6,7},{7,6},{8,9},{9,8},{10,11... | collective-permute-start | bytes 6291464 | tf_op jit(solution)/shard_map/ppermute | solution.py:217
  193.7 89.4 %collective-permute-start.7 = (bf16[1024,1024]{1,0:T(8,128)(2,1)S(1)}, bf16[1024,1024]{1,0:T(8,128)(2,1)S(1)}, u32[]{:S(2)}, u32[]{:S(2)}) collective-permute-start(bf16[1024,1024]{1,0:T(8,128)(2,1)S(1)} %get-tuple-element.127), channel_id=1, source_target_pairs={{0,1},{1,0},{2,3},{3,2},{4,5},{5,4},{6,7},{7,6},{8,9},{9,8},{10,11... | collective-permute-start | bytes 6291464 | tf_op jit(solution)/shard_map/ppermute | solution.py:217
  240.8 42.4 %copy-start.26 = (bf16[1024,1024]{1,0:T(8,128)(2,1)}, bf16[1024,1024]{1,0:T(8,128)(2,1)S(1)}, u32[]{:S(2)}) copy-start(bf16[1024,1024]{1,0:T(8,128)(2,1)S(1)} %collective-permute-done.5) | copy-start | bytes 6291460
  302.6 147.5 %reduce-scatter.13.cloned.1.call-start = ((), (), s32[]{:S(2)}) async-start(), calls=%async_computation.13 | async-start | bytes 1114112 | tf_op jit(solution)/shard_map/reduce_scatter | solution.py:231
  306.9 183.8 %reduce-scatter.11.cloned.1.call-start = ((), (), s32[]{:S(2)}) async-start(), calls=%async_computation.11 | async-start | bytes 3342336 | tf_op jit(solution)/shard_map/reduce_scatter | solution.py:231
  344.9 214.9 %reduce-scatter.9.cloned.1.call-start = ((), (), s32[]{:S(2)}) async-start(), calls=%async_computation.9 | async-start | bytes 3342336 | tf_op jit(solution)/shard_map/reduce_scatter | solution.py:231
  383.0 252.2 %reduce-scatter.17.cloned.1.call-start = ((), (), s32[]{:S(2)}) async-start(), calls=%async_computation.17 | async-start | bytes 4456448 | tf_op jit(solution)/shard_map/reduce_scatter | solution.py:231
  392.5 318.8 %reduce-scatter.19.cloned.1.call-start = ((), (), s32[]{:S(2)}) async-start(), calls=%async_computation.19 | async-start | bytes 4456448 | tf_op jit(solution)/shard_map/reduce_scatter | solution.py:231
  402.2 384.8 %reduce-scatter.21.cloned.1.call-start = ((), (), s32[]{:S(2)}) async-start(), calls=%async_computation.21 | async-start | bytes 4456448 | tf_op jit(solution)/shard_map/reduce_scatter | solution.py:231
  412.5 450.2 %reduce-scatter.23.cloned.1.call-start = ((), (), s32[]{:S(2)}) async-start(), calls=%async_computation.23 | async-start | bytes 4456448 | tf_op jit(solution)/shard_map/reduce_scatter | solution.py:231
  422.0 505.0 %all-reduce.2.cloned.1.call-start = ((), (), s32[]{:S(2)}) async-start(), calls=%async_computation.8 | async-start | bytes 196608 | tf_op jit(solution)/shard_map/psum | solution.py:345
  449.3 523.3 %all-gather.15.cloned.1.call-start = ((), (), s32[]{:S(2)}) async-start(), calls=%async_computation.16 | async-start | bytes 1114112 | tf_op jit(solution)/shard_map/all_gather | solution.py:232
  450.0 522.6 %all-gather.13.cloned.1.call-start = ((), (), s32[]{:S(2)}) async-start(), calls=%async_computation.14 | async-start | bytes 1114112 | tf_op jit(solution)/shard_map/all_gather | solution.py:232
  450.6 536.8 %all-gather.11.cloned.1.call-start = ((), (), s32[]{:S(2)}) async-start(), calls=%async_computation.12 | async-start | bytes 3342336 | tf_op jit(solution)/shard_map/all_gather | solution.py:232
  490.7 542.7 %all-gather.9.cloned.1.call-start = ((), (), s32[]{:S(2)}) async-start(), calls=%async_computation.10 | async-start | bytes 3342336 | tf_op jit(solution)/shard_map/all_gather | solution.py:232
  559.8 524.5 %all-gather.17.cloned.1.call-start = ((), (), s32[]{:S(2)}) async-start(), calls=%async_computation.18 | async-start | bytes 4456448 | tf_op jit(solution)/shard_map/all_gather | solution.py:232
  635.2 500.0 %all-gather.19.cloned.1.call-start = ((), (), s32[]{:S(2)}) async-start(), calls=%async_computation.20 | async-start | bytes 4456448 | tf_op jit(solution)/shard_map/all_gather | solution.py:232
  711.3 474.9 %all-gather.21.cloned.1.call-start = ((), (), s32[]{:S(2)}) async-start(), calls=%async_computation.22 | async-start | bytes 4456448 | tf_op jit(solution)/shard_map/all_gather | solution.py:232
  787.0 450.1 %all-gather.23.cloned.1.call-start = ((), (), s32[]{:S(2)}) async-start(), calls=%async_computation.24 | async-start | bytes 4456448 | tf_op jit(solution)/shard_map/all_gather | solution.py:232
  872.0 26.3 %collective-permute-start.3 = (bf16[512,1024]{1,0:T(8,128)(2,1)}, bf16[512,1024]{1,0:T(8,128)(2,1)}, u32[]{:S(2)}, u32[]{:S(2)}) collective-permute-start(bf16[512,1024]{1,0:T(8,128)(2,1)} %constant_dynamic-slice_fusion.4), channel_id=1, source_target_pairs={{0,1},{1,0},{2,3},{3,2},{4,5},{5,4},{6,7},{7,6},{8,9},{9,8},{10,11... | collective-permute-start | bytes 3145736 | tf_op jit(solution)/shard_map/ppermute | solution.py:225
  878.2 42.6 %copy-start.37 = (f32[1024]{0:T(1024)S(1)}, f32[1024]{0:T(1024)}, u32[]{:S(2)}) copy-start(f32[1024]{0:T(1024)} %param.27) | copy-start | bytes 12292
  879.3 41.5 %collective-permute-start.4 = (bf16[512,1024]{1,0:T(8,128)(2,1)}, bf16[512,1024]{1,0:T(8,128)(2,1)}, u32[]{:S(2)}, u32[]{:S(2)}) collective-permute-start(bf16[512,1024]{1,0:T(8,128)(2,1)} %constant_dynamic-slice_fusion.3), channel_id=1, source_target_pairs={{0,1},{1,0},{2,3},{3,2},{4,5},{5,4},{6,7},{7,6},{8,9},{9,8},{10,11... | collective-permute-start | bytes 3145736 | tf_op jit(solution)/shard_map/ppermute | solution.py:225
  882.3 60.9 %collective-permute-start.8 = (bf16[512,1024]{1,0:T(8,128)(2,1)}, bf16[512,1024]{1,0:T(8,128)(2,1)S(1)}, u32[]{:S(2)}, u32[]{:S(2)}) collective-permute-start(bf16[512,1024]{1,0:T(8,128)(2,1)} %constant_dynamic-slice_fusion.1), channel_id=1, source_target_pairs={{0,1},{1,0},{2,3},{3,2},{4,5},{5,4},{6,7},{7,6},{8,9},{9,8},{10,11... | collective-permute-start | bytes 3145736 | tf_op jit(solution)/shard_map/ppermute | solution.py:225
  883.4 79.7 %collective-permute-start.6 = (bf16[512,1024]{1,0:T(8,128)(2,1)}, bf16[512,1024]{1,0:T(8,128)(2,1)}, u32[]{:S(2)}, u32[]{:S(2)}) collective-permute-start(bf16[512,1024]{1,0:T(8,128)(2,1)} %constant_dynamic-slice_fusion.2), channel_id=1, source_target_pairs={{0,1},{1,0},{2,3},{3,2},{4,5},{5,4},{6,7},{7,6},{8,9},{9,8},{10,11... | collective-permute-start | bytes 3145736 | tf_op jit(solution)/shard_map/ppermute | solution.py:225
  (38 other events, 243.7 us)
Sparse Core Ops, SparseCore 0:
  302.7 58.5 reduce-scatter.14
  364.9 56.5 reduce-scatter.12
  425.3 65.3 reduce-scatter.10
  494.4 65.3 reduce-scatter.8
  563.5 71.6 reduce-scatter.16
  639.5 71.7 reduce-scatter.18
  715.2 71.8 reduce-scatter.20
  790.9 71.8 reduce-scatter.22
  864.9 37.0 all-gather.14
  904.0 36.8 all-gather.12
  943.1 44.2 all-gather.10
  989.5 43.8 all-gather.8
  1035.5 48.6 all-gather.16
  1086.3 48.8 all-gather.18
  1137.3 48.8 all-gather.20
  1188.2 48.8 all-gather.22
Sparse Core Ops, SparseCore 1:
  449.4 136.0 all-reduce.1
